TPU v7x, 512 devices: a whole 4x4x16 slice. The times are simulated.
512 devices in a mesh: dp: 32 (over y, x, core), fsdp: 16 (over z).
Axes of the slice: x: 4, y: 4, z: 16, core: 2. Of those that a mesh axis runs over, the one named last changes fastest.
Arguments:
- queries: bfloat16 [131072, 2048], P(('dp', 'fsdp')), may hold values from -600 to 600
- w_kv: bfloat16 [2, 2048, 896], P(None, 'fsdp'), may hold values from -0.1875 to 0.1875
- encodings: bfloat16 [196608, 896], P(('dp', 'fsdp')), may hold values from -6 to 6
- counts: int32 [512], P(('dp', 'fsdp')), may hold values from 48 to 384, as said below
- owner_rank: int32 [196608], P(('dp', 'fsdp')), may hold values from 0 to 31, as said below
- owner_span: int32 [196608], P(('dp', 'fsdp')), may hold values from 0 to 3, as said below
- grad_ctx: bfloat16 [131072, 2048], P(('dp', 'fsdp')), may hold values from -24 to 24
Outputs:
- grad_queries: bfloat16 [131072, 2048], P(('dp', 'fsdp'))
- grad_value: bfloat16 [2048, 896], P('fsdp')
Inputs may be any that keep to these rules, and one draw needn't show every extreme that they name: `counts`: each count is 384 divided by 1, 2, 4 or 8; among the devices of equal fsdp index one holds 384. `owner_rank`: among the live rows of one device at most 12 name the same owner; a device whose count is 384 names every owner exactly 12 times. `owner_span`: every span of every decoder device is named by at least one live row of a device with equal fsdp index.
All inputs are finite; a program needn't handle non-finite values.
Results may differ from a plain program's by a relative error of at most 0.023.
Values may be sent and summed in bfloat16 or wider, within the bound.
No kernel may reach another device: no remote copies, remote signals or barrier semaphores. Data moves between devices by JAX's collectives and lax.ppermute only.
A program may use at most 64 MiB of HBM per device.

v0:
```python
import jax
import jax.numpy as jnp
from jax import lax
from jax.sharding import PartitionSpec as P

HEADS = 16
HEAD_DIM = 128
SPAN = 64


def total_of_pieces(array, axis):
    return lax.all_gather(array, axis).astype(jnp.float32).sum(0)


def pack_rows(enc_rows, live_count, rank_rows, span_rows, dp_count):
    row_total = enc_rows.shape[0]
    pair_slots = row_total // dp_count
    live_rows = jnp.arange(row_total, dtype=jnp.int32) < live_count
    hit_table = (
        (rank_rows[:, None] == jnp.arange(dp_count, dtype=jnp.int32)[None, :]) & live_rows[:, None]
    ).astype(jnp.int32)
    before_hits = jnp.cumsum(hit_table, axis=0) - hit_table
    slot_index = jnp.sum(before_hits * hit_table, axis=1)
    target = jnp.where(live_rows, rank_rows * pair_slots + slot_index, dp_count * pair_slots)
    buffer = (
        jnp.zeros((dp_count * pair_slots, enc_rows.shape[1]), enc_rows.dtype)
        .at[target]
        .set(enc_rows, mode="drop")
    )
    tag_buffer = (
        jnp.full((dp_count * pair_slots,), -1, jnp.int32).at[target].set(span_rows, mode="drop")
    )
    return (
        buffer.reshape(dp_count, pair_slots, enc_rows.shape[1]),
        tag_buffer.reshape(dp_count, pair_slots),
    )


def local(queries, w_kv, encodings, counts, owner_rank, owner_span, grad_ctx):
    dp_count = lax.axis_size("dp")
    slot_total = encodings.shape[0]
    width = encodings.shape[1]
    buffer, tag_buffer = pack_rows(encodings, counts[0], owner_rank, owner_span, dp_count)
    arrived, arrived_tags = (
        lax.all_to_all(buffer, "dp", split_axis=0, concat_axis=0, tiled=True),
        lax.all_to_all(tag_buffer, "dp", split_axis=0, concat_axis=0, tiled=True),
    )
    received = arrived.reshape(slot_total, width)
    tag_rows = arrived_tags.reshape(slot_total)
    projected = jnp.einsum(
        "re,kne->krn",
        received,
        lax.all_gather(w_kv, "fsdp", axis=1, tiled=True),
        preferred_element_type=jnp.float32,
    ).astype(jnp.bfloat16)
    keys = projected[0]
    values = projected[1]
    token_total = queries.shape[0]
    scale = 1.0 / HEAD_DIM**0.5
    query_heads = queries.reshape(token_total, HEADS, HEAD_DIM)
    key_heads = keys.reshape(slot_total, HEADS, HEAD_DIM)
    value_heads = values.reshape(slot_total, HEADS, HEAD_DIM)
    grad_heads = grad_ctx.reshape(token_total, HEADS, HEAD_DIM)
    scores = (
        jnp.einsum("thd,khd->htk", query_heads, key_heads, preferred_element_type=jnp.float32)
        * scale
    )
    token_span = jnp.arange(token_total, dtype=jnp.int32) // SPAN
    allowed = (token_span[:, None] == tag_rows[None, :])[None]
    masked = jnp.where(allowed, scores, -1e30)
    highest = jnp.max(masked, axis=-1, keepdims=True)
    weights = jnp.where(allowed, jnp.exp(masked - highest), 0.0)
    probs = weights / jnp.sum(weights, axis=-1, keepdims=True)
    probs_low = probs.astype(jnp.bfloat16)
    context = jnp.einsum("htk,khd->thd", probs_low, value_heads, preferred_element_type=jnp.float32)
    dprob = jnp.einsum("thd,khd->htk", grad_heads, value_heads, preferred_element_type=jnp.float32)
    delta = jnp.transpose(jnp.sum(grad_heads.astype(jnp.float32) * context, axis=-1))[:, :, None]
    dscore = (probs * (dprob - delta)).astype(jnp.bfloat16)
    grad_query = (
        jnp.einsum("htk,khd->thd", dscore, key_heads, preferred_element_type=jnp.float32) * scale
    )
    grad_queries = grad_query.astype(jnp.bfloat16).reshape(token_total, HEADS * HEAD_DIM)
    dval = jnp.einsum("htk,thd->khd", probs_low, grad_heads, preferred_element_type=jnp.float32)
    dval = dval.astype(jnp.bfloat16).reshape(slot_total, HEADS * HEAD_DIM)
    shard_sum = lax.psum_scatter(
        lax.dot_general(
            dval, received, (((0,), (0,)), ((), ())), preferred_element_type=jnp.float32
        ).astype(jnp.bfloat16),
        "fsdp",
        scatter_dimension=0,
        tiled=True,
    )
    group_sum = total_of_pieces(shard_sum, "dp").astype(jnp.float32)
    grad_value = (group_sum / dp_count).astype(jnp.bfloat16)
    return (grad_queries, grad_value)


def solution(mesh):
    in_specs = (
        P(("dp", "fsdp"), None),
        P(None, "fsdp", None),
        P(("dp", "fsdp"), None),
        P(("dp", "fsdp")),
        P(("dp", "fsdp")),
        P(("dp", "fsdp")),
        P(("dp", "fsdp"), None),
    )
    out_specs = (P(("dp", "fsdp"), None), P("fsdp", None))
    return jax.shard_map(local, mesh=mesh, in_specs=in_specs, out_specs=out_specs, check_vma=False)
```

profile of v0, /device:TPU:1, one launch (start us, length us, event | category | flops | bytes accessed | tf_op | source)
XLA Modules:
  0.0 291.8 jit_solution(403865007647869411)
XLA Ops:
  7.2 0.0 copy-start
  7.2 0.0 all-gather.4.cloned.1.call-start
  7.2 0.7 all-gather.4.cloned.1.call-update
  8.6 0.7 fusion.26
  9.3 0.9 reduce-window.6
  10.2 0.2 slice_reduce_fusion
  10.4 0.8 fusion.23
  11.2 0.7 compare_select_fusion
  11.9 3.1 %scatter_custom_fusion.1 = s32[384]{0:T(512)S(1)} fusion(s32[384]{0:T(512)S(1)} %compare_select_fusion, s32[384]{0:T(512)} %param.12, s32[]{:T(128)} %constant.40.clone.1), kind=kCustom, calls=%fused_computation.49 | custom fusion | bytes 2048 | tf_op jit(solution)/shard_map/scatter | solution.py:31
  15.0 0.7 all_to_all.10
  15.7 10.3 %all-to-all-start.1 = ((s32[32,1,12]{2,1,0:T(1,128)}), s32[32,1,12]{2,1,0:T(1,128)S(1)}, u32[]{:S(2)}, u32[]{:S(2)}) async-start(s32[32,1,12]{2,1,0:T(1,128)} %bitcast.4), calls=%async_computation.1 | async-start | bytes 32768 | tf_op jit(solution)/shard_map/all_to_all | solution.py:46
  26.0 2.9 scatter_custom_fusion
  28.9 1.1 reshape.101
  30.0 3.0 %all-to-all-done.1 = s32[32,1,12]{2,1,0:T(1,128)S(1)} async-done(((s32[32,1,12]{2,1,0:T(1,128)}), s32[32,1,12]{2,1,0:T(1,128)S(1)}, u32[]{:S(2)}, u32[]{:S(2)}) %all-to-all-start.1) | async-done | bytes 1568 | tf_op jit(solution)/shard_map/all_to_all | solution.py:46
  33.0 4.5 %all-to-all-start = ((bf16[32,12,896]{2,1,0:T(8,128)(2,1)}), bf16[32,12,896]{2,1,0:T(8,128)(2,1)S(1)}, u32[]{:S(2)}, u32[]{:S(2)}) async-start(bf16[32,12,896]{2,1,0:T(8,128)(2,1)} %reshape.101), calls=%async_computation | async-start | bytes 1835008 | tf_op jit(solution)/shard_map/all_to_all | solution.py:45
  37.5 0.2 reduce-scatter.2.cloned.1.call-start
  37.7 1.3 copy.28
  39.1 0.5 broadcast.95
  39.6 0.7 reduce.5
  40.3 0.1 eq.50
  40.4 0.1 broadcast_compare_fusion
  40.5 12.6 %all-to-all-done = bf16[32,12,896]{2,1,0:T(8,128)(2,1)S(1)} async-done(((bf16[32,12,896]{2,1,0:T(8,128)(2,1)}), bf16[32,12,896]{2,1,0:T(8,128)(2,1)S(1)}, u32[]{:S(2)}, u32[]{:S(2)}) %all-to-all-start) | async-done | bytes 688160 | tf_op jit(solution)/shard_map/all_to_all | solution.py:45
  53.1 1.0 reshape.127
  54.1 0.2 reshape.102
  54.3 56.3 %all-gather.4.cloned.1.call-done = bf16[2,2048,896]{2,1,0:T(8,128)(2,1)} async-done(((bf16[2,128,896]{2,1,0:T(8,128)(2,1)}), bf16[2,2048,896]{2,1,0:T(8,128)(2,1)}) %all-gather.4.cloned.1.call-update) | async-done | bytes 7340048 | tf_op jit(solution)/shard_map/all_gather | solution.py:53
  110.6 6.8 %fusion.9 = bf16[2,384,2048]{2,1,0:T(8,128)(2,1)S(1)} fusion(bf16[384,896,1]{1,0,2:T(8,128)(2,1)} %reshape.127, bf16[2,2048,896]{2,1,0:T(8,128)(2,1)} %all-gather.4.cloned.1.call-done), kind=kOutput, calls=%fused_computation.17 | convolution fusion | flops 2820145152 | bytes 11173888 | tf_op jit(solution)/shard_map/re,kne->krn/dot_general | solution.py:50
  117.4 1.5 fusion.31
  118.8 2.6 copy.45
  121.4 0.0 copy-done
  121.4 2.4 fusion.16
  123.9 2.5 fusion.32
  126.4 0.0 copy-start.4
  126.4 0.7 fusion.12
  127.1 1.9 copy-done.2
  129.1 1.6 copy-done.1
  130.7 1.0 convolution_convert_fusion.2
  131.7 4.0 %convolution_convert_fusion = bf16[2048,896]{1,0:T(8,128)(2,1)} fusion(bf16[384,2048]{0,1:T(8,128)(2,1)S(1)} %bitcast.90, bf16[384,896]{1,0:T(8,128)(2,1)S(1)} %reshape.102), kind=kOutput, calls=%fused_computation.9 | convolution fusion | flops 1411121152 | bytes 5931008 | tf_op jit(solution)/shard_map/dot_general | solution.py:86
  135.7 0.0 reduce-scatter.2.cloned.1.call-update
  135.8 0.3 all-gather.6.cloned.1.call-start
  136.0 67.2 %reduce-scatter.2.cloned.1.call-done = bf16[128,896]{1,0:T(8,128)(2,1)} async-done(((bf16[2048,896]{1,0:T(8,128)(2,1)}), bf16[128,896]{1,0:T(8,128)(2,1)}) %reduce-scatter.2.cloned.1.call-update) | async-done | bytes 229392 | tf_op jit(solution)/shard_map/reduce_scatter | solution.py:85
  203.3 0.0 all-gather.6.cloned.1.call-update
  203.3 1.6 copy.46
  204.9 3.5 %fusion.13 = f32[256,16]{0,1:T(8,128)S(1)} fusion(bf16[256,16,128]{0,2,1:T(8,128)(2,1)} %bitcast.85, bf16[384,16,128]{0,2,1:T(8,128)(2,1)} %bitcast.88, bf16[16,256,384]{1,2,0:T(8,128)(2,1)} %copy-done.1), kind=kOutput, calls=%fused_computation.21 | convolution fusion | flops 404221952 | bytes 5783552 | tf_op jit(solution)/shard_map/htk,khd->thd/dot_general | solution.py:75
  208.4 6.5 %multiply_convert_fusion = bf16[16,128,256]{2,1,0:T(8,128)(2,1)} fusion(bf16[384,16,128]{0,2,1:T(8,128)(2,1)S(1)} %bitcast.84, f32[16,256]{1,0:T(8,128)S(1)} %bitcast.94, bf16[384,16,128]{0,2,1:T(8,128)(2,1)} %bitcast.89, bf16[256,16,128]{0,2,1:T(8,128)(2,1)} %bitcast.86, f32[16,256,384]{1,2,0:T(8,128)} %copy-done.2, f32[16,256]{1,0:T(8,128)S(1)} %get-tuple-element.10), kind=kOutput, calls=%fused_computation.22 | convolution fusion | flops 812646400 | bytes 11567104 | tf_op jit(solution)/shard_map/htk,khd->thd/dot_general | solution.py:80
  214.9 2.3 copy.38
  217.1 63.3 %all-gather.6.cloned.1.call-done = bf16[4096,896]{1,0:T(8,128)(2,1)} async-done(((bf16[128,896]{1,0:T(8,128)(2,1)}), bf16[4096,896]{1,0:T(8,128)(2,1)}) %all-gather.6.cloned.1.call-update) | async-done | bytes 7340048 | tf_op jit(solution)/shard_map/all_gather | solution.py:12
  280.4 4.2 %convert_reduce_fusion = f32[128,896]{1,0:T(8,128)S(1)} fusion(bf16[32,128,896]{2,1,0:T(8,128)(2,1)} %bitcast.82), kind=kLoop, calls=%fused_computation.3 | loop fusion | flops 7225344 | bytes 7798784 | tf_op jit(solution)/shard_map/reduce_sum | solution.py:12
  284.5 0.7 multiply_convert_fusion.1
  (11 shorter events, 0.1 us)
Async XLA Ops:
  7.2 114.3 %copy-start = (bf16[256,2048]{1,0:T(8,128)(2,1)S(1)}, bf16[256,2048]{1,0:T(8,128)(2,1)}, u32[]{:S(2)}) copy-start(bf16[256,2048]{1,0:T(8,128)(2,1)} %param.7) | copy-start | bytes 3145732
  7.2 30.6 %copy-start.5 = (bf16[256,2048]{1,0:T(8,128)(2,1)S(1)}, bf16[256,2048]{1,0:T(8,128)(2,1)}, u32[]{:S(2)}) copy-start(bf16[256,2048]{1,0:T(8,128)(2,1)} %param.13) | copy-start | bytes 3145732
  7.2 103.4 %all-gather.4.cloned.1.call-start = ((), (), s32[]{:S(2)}) async-start(), calls=%async_computation.3 | async-start | bytes 7798784 | tf_op jit(solution)/shard_map/all_gather | solution.py:53
  15.7 17.3 %all-to-all-start.1 = ((s32[32,1,12]{2,1,0:T(1,128)}), s32[32,1,12]{2,1,0:T(1,128)S(1)}, u32[]{:S(2)}, u32[]{:S(2)}) async-start(s32[32,1,12]{2,1,0:T(1,128)} %bitcast.4), calls=%async_computation.1 | async-start | bytes 32768 | tf_op jit(solution)/shard_map/all_to_all | solution.py:46
  33.0 20.1 %all-to-all-start = ((bf16[32,12,896]{2,1,0:T(8,128)(2,1)}), bf16[32,12,896]{2,1,0:T(8,128)(2,1)S(1)}, u32[]{:S(2)}, u32[]{:S(2)}) async-start(bf16[32,12,896]{2,1,0:T(8,128)(2,1)} %reshape.101), calls=%async_computation | async-start | bytes 1835008 | tf_op jit(solution)/shard_map/all_to_all | solution.py:45
  37.5 165.8 %reduce-scatter.2.cloned.1.call-start = ((), (), s32[]{:S(2)}) async-start(), calls=%async_computation.4 | async-start | bytes 3899392 | tf_op jit(solution)/shard_map/reduce_scatter | solution.py:85
  126.4 2.7 copy-start.2
  126.4 4.3 %copy-start.4 = (bf16[256,2048]{0,1:T(8,128)(2,1)S(1)}, bf16[256,2048]{0,1:T(8,128)(2,1)}, u32[]{:S(2)}) copy-start(bf16[256,2048]{0,1:T(8,128)(2,1)} %copy.28) | copy-start | bytes 3145732
  129.1 1.6 copy-start.1
  135.8 144.6 %all-gather.6.cloned.1.call-start = ((), (), s32[]{:S(2)}) async-start(), calls=%async_computation.5 | async-start | bytes 7569408 | tf_op jit(solution)/shard_map/all_gather | solution.py:12
  204.9 3.5 %copy-start.3 = (bf16[1,384,2048]{1,2,0:T(8,128)(2,1)S(1)}, bf16[1,384,2048]{1,2,0:T(8,128)(2,1)}, u32[]{:S(2)}) copy-start(bf16[1,384,2048]{1,2,0:T(8,128)(2,1)} %copy.45) | copy-start | bytes 4718596
Sparse Core Ops, SparseCore 0:
  10.1 100.4 all-gather.3
  135.9 67.3 reduce-scatter.1
  206.4 73.9 all-gather.5
where the time goes:
time: 292 us
  waiting for transfers between devices  203 us (70%)
  matrix products  24.1 us (8%)
  local copies, waits for them, and re-layouts  22.6 us (8%)
  starting transfers between devices  15.3 us (5%)
  between operations  14.6 us (5%)
  other arithmetic  12 us (4%)
    reduce_scatter x1, waiting for transfers between devices, local(): lax.psum_scatter(lax.dot_general(dval, received, (((0,), (0,)), ((), ()))...  67.2 us
    all_gather x1, waiting for transfers between devices, total_of_pieces(): return lax.all_gather(array, axis).astype(jnp.float32).sum(0)  63.3 us
    all_gather x1, waiting for transfers between devices, local(): lax.all_gather(w_kv, 'fsdp', axis=1, tiled=True)  56.3 us
    all_to_all x1, waiting for transfers between devices, local(): lax.all_to_all(buffer, 'dp', split_axis=0, concat_axis=0, tiled=True)  12.6 us
    all_to_all x1, starting transfers between devices, local(): lax.all_to_all(tag_buffer, 'dp', split_axis=0, concat_axis=0, tiled=True)  10.3 us
    unnamed x14, local copies, waits for them, and re-layouts  7.19 us
    dot_general x1, matrix products, local(): jnp.einsum('re,kne->krn', received, lax.all_gather(w_kv, 'fsdp', axis=1,...  6.76 us
    dot_general x1, matrix products, local(): jnp.einsum('htk,khd->thd', dscore, key_heads, preferred_element_type=jnp....  6.48 us
  transfers between devices with their start and end apart: 5, of which 5 were waited for; matrix products, arithmetic and copies ran while one was open for 10% of the time, Pallas kernels for 0%

commit v1 on v0

--- a/solution.py
+++ b/solution.py
@@ -6,6 +6,11 @@
 HEADS = 16
 HEAD_DIM = 128
 SPAN = 64
+
+
+def gather_over(shard, axis, d):
+    sent = jnp.stack([shard] * lax.axis_size(axis))
+    return jnp.concatenate(lax.all_to_all(sent, axis, 0, 0), axis=d)
 
 
 def total_of_pieces(array, axis):
@@ -48,10 +53,7 @@
     received = arrived.reshape(slot_total, width)
     tag_rows = arrived_tags.reshape(slot_total)
     projected = jnp.einsum(
-        "re,kne->krn",
-        received,
-        lax.all_gather(w_kv, "fsdp", axis=1, tiled=True),
-        preferred_element_type=jnp.float32,
+        "re,kne->krn", received, gather_over(w_kv, "fsdp", 1), preferred_element_type=jnp.float32
     ).astype(jnp.bfloat16)
     keys = projected[0]
     values = projected[1]

time: 292 us -> 570 us (1.95)
  waiting for transfers between devices: 203 us -> 448 us
  blocking collectives: 0 us -> 19.4 us
  starting transfers between devices: 15.3 us -> 24 us
  local copies, waits for them, and re-layouts: 22.6 us -> 29.9 us
    all_to_all x1, waiting for transfers between devices: 12.6 us -> 312 us  [gather_over(): return jnp.concatenate(lax.all_to_all(sent, axis, 0, 0), axis=d)]
    all_gather x1 -> x0, waiting for transfers between devices: 56.3 us -> none  [local(): lax.all_gather(w_kv, 'fsdp', axis=1, tiled=True)]
    all_to_all x0 -> x1, blocking collectives: none -> 19.4 us  [local(): lax.all_to_all(buffer, 'dp', split_axis=0, concat_axis=0, tiled=True)]
    all_to_all x1, starting transfers between devices: 4.48 us -> 13.2 us  [gather_over(): return jnp.concatenate(lax.all_to_all(sent, axis, 0, 0), axis=d)]
  transfers between devices with their start and end apart: 5 -> 4, of which waited for: 5 -> 4; matrix products, arithmetic and copies ran while one was open for 10% -> 4% of each run, Pallas kernels for 0% -> 0%
where the time goes in v1:
time: 570 us; the launch traced here: 569 us
  waiting for transfers between devices  448 us (79%)
  local copies, waits for them, and re-layouts  29.9 us (5%)
  starting transfers between devices  24 us (4%)
  matrix products  20.5 us (4%)
  blocking collectives  19.4 us (3%)
  between operations  15 us (3%)
  other arithmetic  12.1 us (2%)
    all_to_all x1, waiting for transfers between devices, gather_over(): return jnp.concatenate(lax.all_to_all(sent, axis, 0, 0), axis=d)  312 us
    reduce_scatter x1, waiting for transfers between devices, local(): lax.psum_scatter(lax.dot_general(dval, received, (((0,), (0,)), ((), ()))...  68.1 us
    all_gather x1, waiting for transfers between devices, total_of_pieces(): return lax.all_gather(array, axis).astype(jnp.float32).sum(0)  63.8 us
    all_to_all x1, blocking collectives, local(): lax.all_to_all(buffer, 'dp', split_axis=0, concat_axis=0, tiled=True)  19.4 us
    all_to_all x1, starting transfers between devices, gather_over(): return jnp.concatenate(lax.all_to_all(sent, axis, 0, 0), axis=d)  13.2 us
  transfers between devices with their start and end apart: 4, of which 4 were waited for; matrix products, arithmetic and copies ran while one was open for 4% of the time, Pallas kernels for 0%

profile of v1, /device:TPU:1, one launch (start us, length us, event | category | flops | bytes accessed | tf_op | source)
XLA Modules:
  0.0 569.2 jit_solution(12969901780030397876)
XLA Ops:
  7.2 0.0 copy-start
  7.2 0.0 copy-start.8
  8.0 0.7 fusion.26
  8.7 0.9 reduce-window.6
  9.5 0.2 slice_reduce_fusion
  9.8 0.8 fusion.23
  10.6 0.7 compare_select_fusion
  11.3 3.1 scatter_custom_fusion.1
  14.4 0.7 all_to_all.14
  15.1 10.3 %all-to-all-start.2 = ((s32[32,1,12]{2,1,0:T(1,128)}), s32[32,1,12]{2,1,0:T(1,128)S(1)}, u32[]{:S(2)}, u32[]{:S(2)}) async-start(s32[32,1,12]{2,1,0:T(1,128)} %bitcast.6), calls=%async_computation.2 | async-start | bytes 32768 | tf_op jit(solution)/shard_map/all_to_all | solution.py:51
  25.4 2.9 scatter_custom_fusion
  28.3 0.2 reshape.109
  28.5 3.9 all-to-all-done.2
  32.4 19.4 %all_to_all.19 = bf16[32,12,896]{2,1,0:T(8,128)(2,1)S(1)} all-to-all(bf16[32,12,896]{2,1,0:T(8,128)(2,1)S(1)} %reshape.109), channel_id=1, replica_groups=mesh['dp'=32,'fsdp'=16] {'dp'}, dimensions={0} | all-to-all | bytes 1376256 | tf_op jit(solution)/shard_map/all_to_all | solution.py:50
  51.8 4.1 stack.2
  55.8 13.2 %all-to-all-start.1 = ((bf16[16,2,128,896]{3,2,1,0:T(8,128)(2,1)}), bf16[16,2,128,896]{3,2,1,0:T(8,128)(2,1)}, u32[]{:S(2)}, u32[]{:S(2)}) async-start(bf16[16,2,128,896]{3,2,1,0:T(8,128)(2,1)} %stack.2), calls=%async_computation.1 | async-start | bytes 14680064 | tf_op jit(solution)/shard_map/all_to_all | solution.py:13
  69.1 0.2 reduce-scatter.2.cloned.1.call-start
  69.3 1.3 copy.29
  70.6 0.5 broadcast.97
  71.1 0.7 reduce.5
  71.8 0.1 eq.50
  71.9 0.1 broadcast_compare_fusion
  72.1 1.0 reshape.137
  73.1 0.2 reshape.110
  73.3 312.5 %all-to-all-done.1 = bf16[16,2,128,896]{3,2,1,0:T(8,128)(2,1)} async-done(((bf16[16,2,128,896]{3,2,1,0:T(8,128)(2,1)}), bf16[16,2,128,896]{3,2,1,0:T(8,128)(2,1)}, u32[]{:S(2)}, u32[]{:S(2)}) %all-to-all-start.1) | async-done | bytes 7340064 | tf_op jit(solution)/shard_map/all_to_all | solution.py:13
  385.8 4.1 copy.25
  389.9 3.7 fusion.9
  393.6 1.5 fusion.31
  395.0 2.6 copy.46
  397.6 2.4 fusion.16
  400.1 2.5 fusion.32
  402.6 0.0 copy-start.5
  402.6 0.7 fusion.12
  403.3 1.9 copy-done.3
  405.3 1.6 copy-done.2
  406.9 1.0 convolution_convert_fusion.2
  407.9 4.0 convolution_convert_fusion
  411.9 0.0 reduce-scatter.2.cloned.1.call-update
  412.0 0.3 all-gather.3.cloned.1.call-start
  412.2 68.1 %reduce-scatter.2.cloned.1.call-done = bf16[128,896]{1,0:T(8,128)(2,1)} async-done(((bf16[2048,896]{1,0:T(8,128)(2,1)}), bf16[128,896]{1,0:T(8,128)(2,1)}) %reduce-scatter.2.cloned.1.call-update) | async-done | bytes 229392 | tf_op jit(solution)/shard_map/reduce_scatter | solution.py:87
  480.3 0.0 all-gather.3.cloned.1.call-update
  480.3 1.6 copy.47
  481.9 3.2 fusion.13
  485.1 6.2 %multiply_convert_fusion = bf16[16,128,256]{2,1,0:T(8,128)(2,1)} fusion(bf16[384,16,128]{0,2,1:T(8,128)(2,1)S(1)} %bitcast.87, f32[16,256]{1,0:T(8,128)S(1)} %bitcast.97, bf16[384,16,128]{0,2,1:T(8,128)(2,1)} %bitcast.92, bf16[256,16,128]{0,2,1:T(8,128)(2,1)S(1)} %bitcast.90, f32[16,256,384]{1,2,0:T(8,128)} %copy-done.3, f32[16,256]{1,0:T(8,128)S(1)} %get-tuple-element.10), kind=kOutput, calls=%fused_computation.22 | convolution fusion | flops 812646400 | bytes 11567104 | tf_op jit(solution)/shard_map/htk,khd->thd/dot_general | solution.py:82
  491.3 2.3 copy.39
  493.6 63.8 %all-gather.3.cloned.1.call-done = bf16[4096,896]{1,0:T(8,128)(2,1)} async-done(((bf16[128,896]{1,0:T(8,128)(2,1)}), bf16[4096,896]{1,0:T(8,128)(2,1)}) %all-gather.3.cloned.1.call-update) | async-done | bytes 7340048 | tf_op jit(solution)/shard_map/all_gather | solution.py:17
  557.4 4.2 convert_reduce_fusion
  561.6 0.7 multiply_convert_fusion.1
  (17 shorter events, 0.1 us)
Async XLA Ops:
  7.2 390.5 %copy-start = (bf16[256,2048]{1,0:T(8,128)(2,1)S(1)}, bf16[256,2048]{1,0:T(8,128)(2,1)}, u32[]{:S(2)}) copy-start(bf16[256,2048]{1,0:T(8,128)(2,1)} %param.7) | copy-start | bytes 3145732
  7.2 44.6 %copy-start.8 = (bf16[2,128,896]{2,1,0:T(8,128)(2,1)S(1)}, bf16[2,128,896]{2,1,0:T(8,128)(2,1)}, u32[]{:S(2)}) copy-start(bf16[2,128,896]{2,1,0:T(8,128)(2,1)} %param.8) | copy-start | bytes 1376260
  15.1 17.3 %all-to-all-start.2 = ((s32[32,1,12]{2,1,0:T(1,128)}), s32[32,1,12]{2,1,0:T(1,128)S(1)}, u32[]{:S(2)}, u32[]{:S(2)}) async-start(s32[32,1,12]{2,1,0:T(1,128)} %bitcast.6), calls=%async_computation.2 | async-start | bytes 32768 | tf_op jit(solution)/shard_map/all_to_all | solution.py:51
  55.8 13.5 %copy-start.6 = (bf16[256,2048]{1,0:T(8,128)(2,1)S(1)}, bf16[256,2048]{1,0:T(8,128)(2,1)}, u32[]{:S(2)}) copy-start(bf16[256,2048]{1,0:T(8,128)(2,1)} %param.13) | copy-start | bytes 3145732
  55.8 329.9 %all-to-all-start.1 = ((bf16[16,2,128,896]{3,2,1,0:T(8,128)(2,1)}), bf16[16,2,128,896]{3,2,1,0:T(8,128)(2,1)}, u32[]{:S(2)}, u32[]{:S(2)}) async-start(bf16[16,2,128,896]{3,2,1,0:T(8,128)(2,1)} %stack.2), calls=%async_computation.1 | async-start | bytes 14680064 | tf_op jit(solution)/shard_map/all_to_all | solution.py:13
  69.1 411.2 %reduce-scatter.2.cloned.1.call-start = ((), (), s32[]{:S(2)}) async-start(), calls=%async_computation.4 | async-start | bytes 3899392 | tf_op jit(solution)/shard_map/reduce_scatter | solution.py:87
  385.8 4.1 copy-start.7
  402.6 2.7 copy-start.3
  402.6 4.3 copy-start.5
  405.3 1.6 copy-start.2
  412.0 145.4 %all-gather.3.cloned.1.call-start = ((), (), s32[]{:S(2)}) async-start(), calls=%async_computation.5 | async-start | bytes 7569408 | tf_op jit(solution)/shard_map/all_gather | solution.py:17
  481.9 3.2 copy-start.4
  557.4 5.0 copy-start.1
Sparse Core Ops, SparseCore 0:
  412.1 68.1 reduce-scatter.1
  483.4 73.8 all-gather.2
